TPU v7x, 32 devices: a whole 2x2x4 slice. The times are simulated.
32 devices in a mesh: pass: 16 (over z, y, core), voc: 2 (over x).
Axes of the slice: x: 2, y: 2, z: 4, core: 2. Of those that a mesh axis runs over, the one named last changes fastest.
Arguments:
- hidden: bfloat16 [512, 16, 768], P('pass'), may hold values from -6 to 6
- positions: int32 [512, 8], P('pass'), may hold values from 0 to 15
- passage_weight: float32 [512], P('pass'), may hold values from 0.4 to 2.5
- passage_counts: int32 [32], replicated, may hold values from 1 to 24, 512 in all
- passage_slot: int32 [512], replicated, may hold values from 0 to 511, each once
- head_weight: bfloat16 [768, 30720], P(None, 'voc'), may hold values from -0.21875 to 0.21875
- head_bias: float32 [30720], P('voc'), may hold values from -5 to 5
- queries: bfloat16 [32, 30720], P('pass', 'voc'), may hold values from -1 to 1
Outputs:
- scores: float32 [32, 32], P('pass')
- hidden_grad: bfloat16 [512, 16, 768], P('pass')
Inputs may be any that keep to these rules, and one draw needn't show every extreme that they name: `passage_slot`: each slot holds exactly one passage.
All inputs are finite; a program needn't handle non-finite values.
Results may differ from a plain program's by a relative error of at most 0.015.
Values may be sent and summed in bfloat16 or wider, within the bound.
No kernel may reach another device: no remote copies, remote signals or barrier semaphores. Data moves between devices by JAX's collectives and lax.ppermute only.
A program may use at most 128 MiB of HBM per device.

v0:
```python
import jax
import jax.numpy as jnp
from jax import lax
from jax.sharding import PartitionSpec as P

HIGH = lax.Precision.HIGHEST


def vocab_total(partial_value):
    return lax.psum(partial_value, "voc")


def score_gradient(scores, owned, doc_total):
    query_first = lax.axis_index("pass") * owned
    rows = query_first + jnp.arange(owned, dtype=jnp.int32)
    target = (jnp.arange(doc_total, dtype=jnp.int32)[None, :] == rows[:, None]).astype(jnp.float32)
    prob = jax.nn.softmax(scores, axis=1)
    return (prob - target) / doc_total


def on_device(
    hidden, positions, passage_weight, passage_counts, passage_slot, head_weight, head_bias, queries
):
    count = hidden.shape[0]
    seq_len = hidden.shape[1]
    width = hidden.shape[2]
    picks = positions.shape[1]
    total = passage_slot.shape[0]
    doc_total = passage_counts.shape[0]
    owned = queries.shape[0]
    vocab_local = head_weight.shape[1]
    ends = jnp.cumsum(passage_counts)
    order = jnp.arange(total, dtype=jnp.int32)
    doc_order = jnp.sum((ends[None, :] <= order[:, None]).astype(jnp.int32), axis=1)
    local_slot = lax.axis_index("pass") * count + jnp.arange(count, dtype=jnp.int32)
    matched = passage_slot[None, :] == local_slot[:, None]
    doc_local = jnp.sum(jnp.where(matched, doc_order[None, :], 0), axis=1)
    mixing = jnp.where(
        doc_local[None, :] == jnp.arange(doc_total, dtype=jnp.int32)[:, None],
        passage_weight[None, :],
        jnp.float32(0.0),
    )
    picked = jax.vmap(lambda h, p: h[p])(hidden, positions).reshape(-1, width)
    logits = jnp.dot(picked, head_weight, preferred_element_type=jnp.float32) + head_bias
    active = jnp.log1p(jnp.maximum(logits, 0.0))
    rep = active.reshape(count, picks, vocab_local).sum(axis=1).astype(jnp.bfloat16)
    all_queries = lax.all_gather(queries, "pass", axis=0, tiled=True)
    paired = lax.dot_general(
        all_queries, rep, (((1,), (1,)), ((), ())), preferred_element_type=jnp.float32
    )
    parts = lax.dot_general(paired, mixing, (((1,), (1,)), ((), ())), precision=HIGH)
    scores = vocab_total(lax.psum_scatter(parts, "pass", scatter_dimension=0, tiled=True))
    dscore = score_gradient(scores, owned, doc_total)
    all_dscore = lax.all_gather(dscore, "pass", axis=0, tiled=True)
    per_query = lax.dot_general(mixing, all_dscore, (((0,), (1,)), ((), ())), precision=HIGH)
    drep = jnp.dot(per_query, all_queries.astype(jnp.float32), precision=HIGH)
    shaped = logits.reshape(count, picks, vocab_local)
    growth = 1.0 + jnp.maximum(shaped, 0.0)
    dlogits = jnp.where(shaped > 0, drep[:, None, :] / growth, jnp.float32(0.0)).astype(
        jnp.bfloat16
    )
    token_part = lax.dot_general(
        dlogits.reshape(-1, vocab_local),
        head_weight,
        (((1,), (1,)), ((), ())),
        preferred_element_type=jnp.float32,
    )
    dpicked = lax.psum(token_part.astype(jnp.bfloat16), "voc").astype(jnp.float32)
    onehot = (positions[:, :, None] == jnp.arange(seq_len, dtype=jnp.int32)[None, None, :]).astype(
        jnp.float32
    )
    hidden_grad = jnp.einsum(
        "bps,bpd->bsd", onehot, dpicked.reshape(count, picks, width), precision=HIGH
    )
    return (scores, hidden_grad.astype(jnp.bfloat16))


def solution(mesh):
    placed = (
        P("pass", None, None),
        P("pass", None),
        P("pass"),
        P(),
        P(),
        P(None, "voc"),
        P("voc"),
        P("pass", "voc"),
    )
    return jax.shard_map(
        on_device,
        mesh=mesh,
        in_specs=placed,
        out_specs=(P("pass", None), P("pass", None, None)),
        check_vma=False,
    )
```

profile of v0, /device:TPU:0, one launch (start us, length us, event | category | flops | bytes accessed | tf_op | source)
XLA Modules:
  0.0 201.1 jit_solution(16383369175153553843)
XLA Ops:
  7.2 0.0 copy-start
  7.2 0.0 all-reduce.3.cloned.1.call-start
  7.2 0.8 fusion.26
  8.0 0.1 copy.18
  8.1 0.1 reshape.62
  8.2 26.2 %all-gather = bf16[16,2,15360]{2,1,0:T(2,128)(2,1)S(1)} all-gather(bf16[1,2,15360]{2,1,0:T(2,128)(2,1)} %bitcast.38), channel_id=1, replica_groups=mesh['pass'=16,'voc'=2] {'pass'}, dimensions={0}, use_global_device_ids=true | all-gather | bytes 1044480 | tf_op jit(solution)/shard_map/all_gather | solution.py:47
  34.4 0.4 reshape.75
  34.8 0.7 copy.19
  35.5 0.1 reduce-window.8
  35.6 0.1 reduce
  35.7 0.1 convert_reduce_fusion
  35.8 0.0 copy-done
  35.8 2.4 %gather_fusion = bf16[256,768]{1,0:T(8,128)(2,1)S(1)} fusion(bf16[32,16,768]{2,1,0:T(8,128)(2,1)S(1)} %copy-done, s32[256]{0:T(256)S(1)} %reshape.62), kind=kCustom, calls=%fused_computation | custom fusion | bytes 788480 | tf_op jit(solution)/shard_map/vmap()/gather | solution.py:43
  38.2 0.0 copy-start.4
  38.2 0.0 copy-start.3
  38.3 0.0 copy-start.5
  38.3 27.2 %bitcast_reduce_fusion = (bf16[32,15360]{1,0:T(8,128)(2,1)S(1)}, f32[256,15360]{1,0:T(8,128)}) fusion(f32[15360]{0:T(1024)} %param.14, bf16[256,768]{1,0:T(8,128)(2,1)S(1)} %gather_fusion, bf16[768,15360]{1,0:T(8,128)(2,1)} %param.13), kind=kOutput, calls=%fused_computation.5 | convolution fusion | flops 6051102720 | bytes 40759296 | tf_op jit(solution)/shard_map/dot_general | solution.py:44
  65.5 0.4 fusion.33
  65.9 0.0 copy-done.4
  65.9 0.2 select_reduce_fusion
  66.1 0.0 copy-done.3
  66.1 0.2 fusion.15
  66.3 57.8 %all-reduce = f32[32,32]{1,0:T(8,128)S(1)} all-reduce(f32[32,32]{1,0:T(8,128)S(1)} %fusion.15), channel_id=2, replica_groups=mesh['pass'=16,'voc'=2] {'pass'}, use_global_device_ids=true, to_apply=%region_4.5.clone | all-reduce | flops 1024 | bytes 8192
  124.1 0.0 copy-done.5
  124.2 0.6 dynamic-slice
  125.4 4.9 %psum.14 = f32[2,32]{1,0:T(2,128)S(1)} all-reduce(f32[2,32]{1,0:T(2,128)S(1)} %constant_dynamic-slice_fusion), channel_id=1, replica_groups=mesh['pass'=16,'voc'=2] {'voc'}, use_global_device_ids=true, to_apply=%region_5.6 | all-reduce | flops 64 | bytes 512 | tf_op jit(solution)/shard_map/psum | solution.py:10
  130.3 0.0 copy-start.2
  130.3 0.1 reduce_max.9
  130.5 0.2 fusion.27
  130.6 0.1 multiply_bitcast_fusion
  130.7 17.3 %all-gather.1 = f32[16,2,32]{2,1,0:T(2,128)S(1)} all-gather(f32[1,2,32]{2,1,0:T(2,128)S(1)} %multiply_bitcast_fusion), channel_id=1, replica_groups=mesh['pass'=16,'voc'=2] {'pass'}, dimensions={0}, use_global_device_ids=true | all-gather | bytes 4352 | tf_op jit(solution)/shard_map/all_gather | solution.py:54
  148.1 0.2 fusion.13
  148.3 2.2 %fusion.32 = f32[32,15360]{1,0:T(8,128)} fusion(f32[32,32]{1,0:T(8,128)S(1)} %fusion.13, bf16[32,15360]{1,0:T(8,128)(2,1)S(1)} %reshape.75), kind=kOutput, calls=%fused_computation.45 | convolution fusion | flops 188743680 | bytes 2953216 | tf_op jit(solution)/shard_map/dot_general | solution.py:56
  150.5 0.0 copy-start.1
  150.5 16.6 %fusion.7 = bf16[32,8,768]{2,1,0:T(8,128)(2,1)} fusion(bf16[768,15360]{1,0:T(8,128)(2,1)} %param.13, f32[256,15360]{1,0:T(8,128)} %get-tuple-element.3, f32[32,15360]{1,0:T(8,128)} %fusion.32), kind=kOutput, calls=%fused_computation.9 | convolution fusion | flops 6063587328 | bytes 41680896 | tf_op jit(solution)/shard_map/dot_general | solution.py:62
  167.0 0.0 copy-done.2
  167.0 0.0 all-reduce.3.cloned.1.call-update
  167.1 0.0 copy-done.1
  167.1 0.1 copy.20
  167.1 24.5 %all-reduce.3.cloned.1.call-done = bf16[32,8,768]{2,1,0:T(8,128)(2,1)} async-done(((bf16[32,8,768]{2,1,0:T(8,128)(2,1)}), bf16[32,8,768]{2,1,0:T(8,128)(2,1)}) %all-reduce.3.cloned.1.call-update) | async-done | bytes 393232 | tf_op jit(solution)/shard_map/psum | solution.py:68
  191.7 2.6 %convolution_convert_fusion = bf16[32,16,768]{2,1,0:T(8,128)(2,1)} fusion(bf16[32,8,768]{2,1,0:T(8,128)(2,1)} %all-reduce.3.cloned.1.call-done, s32[32,8]{1,0:T(8,128)S(1)} %copy.20), kind=kOutput, calls=%fused_computation.7 | convolution fusion | flops 6688768 | bytes 1180672 | tf_op jit(solution)/shard_map/bps,bpd->bsd/dot_general | solution.py:72
  (3 shorter events, 0.0 us)
Async XLA Ops:
  7.2 28.6 %copy-start = (bf16[32,16,768]{2,1,0:T(8,128)(2,1)S(1)}, bf16[32,16,768]{2,1,0:T(8,128)(2,1)}, u32[]{:S(2)}) copy-start(bf16[32,16,768]{2,1,0:T(8,128)(2,1)} %param.8) | copy-start | bytes 2359300
  7.2 184.5 %all-reduce.3.cloned.1.call-start = ((), (), s32[]{:S(2)}) async-start(), calls=%async_computation | async-start | bytes 786432 | tf_op jit(solution)/shard_map/psum | solution.py:68
  38.2 27.7 %copy-start.4 = (s32[512]{0:T(512)S(1)}, s32[512]{0:T(512)}, u32[]{:S(2)}) copy-start(s32[512]{0:T(512)} %param.12) | copy-start | bytes 6148
  38.2 27.9 %copy-start.3 = (f32[32]{0:T(128)S(1)}, f32[32]{0:T(128)}, u32[]{:S(2)}) copy-start(f32[32]{0:T(128)} %param.10) | copy-start | bytes 388
  38.3 85.9 %copy-start.5 = (u32[32]{0:T(128)S(1)}, u32[32]{0:T(128)}, u32[]{:S(2)}) copy-start(u32[32]{0:T(128)} %constant.46) | copy-start | bytes 388
  130.3 36.7 %copy-start.2 = (f32[2,32]{1,0:T(2,128)}, f32[2,32]{1,0:T(2,128)S(1)}, u32[]{:S(2)}) copy-start(f32[2,32]{1,0:T(2,128)S(1)} %psum.14) | copy-start | bytes 772
  150.5 16.6 %copy-start.1 = (s32[32,8]{0,1:T(8,128)S(1)}, s32[32,8]{0,1:T(8,128)}, u32[]{:S(2)}) copy-start(s32[32,8]{0,1:T(8,128)} %param.9) | copy-start | bytes 3076
Sparse Core Ops, SparseCore 0:
  167.2 24.4 all-reduce.2
where the time goes:
time: 201 us
  blocking collectives  106 us (53%)
  matrix products  49.4 us (25%)
  waiting for transfers between devices  24.5 us (12%)
  between operations  14.8 us (7%)
  local copies, waits for them, and re-layouts  4.4 us (2%)
    unnamed x1, blocking collectives  57.8 us
    dot_general x1, matrix products, on_device(): jnp.dot(picked, head_weight, preferred_element_type=jnp.float32) + head_bias  27.2 us
    all_gather x1, blocking collectives, on_device(): all_queries = lax.all_gather(queries, 'pass', axis=0, tiled=True)  26.2 us
    psum x1, waiting for transfers between devices, on_device(): lax.psum(token_part.astype(jnp.bfloat16), 'voc').astype(jnp.float32)  24.5 us
    all_gather x1, blocking collectives, on_device(): all_dscore = lax.all_gather(dscore, 'pass', axis=0, tiled=True)  17.3 us
    dot_general x1, matrix products, on_device(): lax.dot_general(dlogits.reshape(-1, vocab_local), head_weight, (((1,), (1...  16.6 us
    psum x1, blocking collectives, vocab_total(): return lax.psum(partial_value, 'voc')  4.93 us
  transfers between devices with their start and end apart: 1, of which 1 were waited for; matrix products, arithmetic and copies ran while one was open for 0% of the time, Pallas kernels for 0%

commit v1 on v0

--- a/solution.py
+++ b/solution.py
@@ -51,7 +51,17 @@
     parts = lax.dot_general(paired, mixing, (((1,), (1,)), ((), ())), precision=HIGH)
     scores = vocab_total(lax.psum_scatter(parts, "pass", scatter_dimension=0, tiled=True))
     dscore = score_gradient(scores, owned, doc_total)
-    all_dscore = lax.all_gather(dscore, "pass", axis=0, tiled=True)
+    inputs = dscore
+    val = lax.axis_size("pass")
+    then, a_now, carry_out = (val, lax.axis_index("pass"), inputs.shape[0])
+    shelf = [to_i * then if at == 0 else to_i for at, to_i in enumerate(inputs.shape)]
+    last = jnp.zeros(shelf, inputs.dtype)
+    all_dscore = lax.dynamic_update_slice_in_dim(last, inputs, a_now * carry_out, axis=0)
+    for b in range(1, then):
+        inputs = lax.ppermute(inputs, "pass", [(at, (at + 1) % then) for at in range(then)])
+        all_dscore = lax.dynamic_update_slice_in_dim(
+            all_dscore, inputs, (a_now - b) % then * carry_out, axis=0
+        )
     per_query = lax.dot_general(mixing, all_dscore, (((0,), (1,)), ((), ())), precision=HIGH)
     drep = jnp.dot(per_query, all_queries.astype(jnp.float32), precision=HIGH)
     shaped = logits.reshape(count, picks, vocab_local)

time: 201 us -> 267 us (1.33)
  waiting for transfers between devices: 24.5 us -> 108 us
  blocking collectives: 106 us -> 89 us
    ppermute x0 -> x15, waiting for transfers between devices: none -> 85 us  [on_device(): lax.ppermute(inputs, 'pass', [(at, (at + 1) % then) for at in range(then)])]
    all_gather x1 -> x0, blocking collectives: 17.3 us -> none  [on_device(): all_dscore = lax.all_gather(dscore, 'pass', axis=0, tiled=True)]
  transfers between devices with their start and end apart: 1 -> 16, of which waited for: 1 -> 16; matrix products, arithmetic and copies ran while one was open for 0% -> 0% of each run, Pallas kernels for 0% -> 0%
where the time goes in v1:
time: 267 us; the launch traced here: 266 us
  waiting for transfers between devices  108 us (40%)
  blocking collectives  89 us (33%)
  matrix products  47.8 us (18%)
  between operations  15.2 us (6%)
  local copies, waits for them, and re-layouts  4.51 us (2%)
    ppermute x15, waiting for transfers between devices, on_device(): lax.ppermute(inputs, 'pass', [(at, (at + 1) % then) for at in range(then)])  85 us
    unnamed x1, blocking collectives  57.8 us
    dot_general x1, matrix products, on_device(): jnp.dot(picked, head_weight, preferred_element_type=jnp.float32) + head_bias  27.4 us
    all_gather x1, blocking collectives, on_device(): all_queries = lax.all_gather(queries, 'pass', axis=0, tiled=True)  26.2 us
    psum x1, waiting for transfers between devices, on_device(): lax.psum(token_part.astype(jnp.bfloat16), 'voc').astype(jnp.float32)  23.1 us
    dot_general x1, matrix products, on_device(): lax.dot_general(dlogits.reshape(-1, vocab_local), head_weight, (((1,), (1...  16.1 us
  transfers between devices with their start and end apart: 16, of which 16 were waited for; matrix products, arithmetic and copies ran while one was open for 0% of the time, Pallas kernels for 0%

profile of v1, /device:TPU:0, one launch (start us, length us, event | category | flops | bytes accessed | tf_op | source)
XLA Modules:
  0.0 266.3 jit_solution(13825186493736311001)
XLA Ops:
  7.2 0.0 copy-start
  7.2 0.0 all-reduce.3.cloned.1.call-start
  7.2 0.8 fusion.26
  8.0 0.1 copy.18
  8.1 0.1 reshape.62
  8.2 26.2 %all-gather = bf16[16,2,15360]{2,1,0:T(2,128)(2,1)S(1)} all-gather(bf16[1,2,15360]{2,1,0:T(2,128)(2,1)} %bitcast.34), channel_id=1, replica_groups=mesh['pass'=16,'voc'=2] {'pass'}, dimensions={0}, use_global_device_ids=true | all-gather | bytes 1044480 | tf_op jit(solution)/shard_map/all_gather | solution.py:47
  34.4 0.4 reshape.75
  34.8 0.7 copy.19
  35.5 0.1 reduce-window.8
  35.6 0.1 reduce
  35.7 0.1 convert_reduce_fusion
  35.8 2.4 gather_fusion
  38.2 0.0 copy-start.4
  38.3 0.0 copy-start.5
  38.3 27.4 %bitcast_reduce_fusion = (bf16[32,15360]{1,0:T(8,128)(2,1)S(1)}, f32[256,15360]{1,0:T(8,128)}) fusion(f32[15360]{0:T(1024)} %param.14, bf16[256,768]{1,0:T(8,128)(2,1)S(1)} %gather_fusion, bf16[768,15360]{1,0:T(8,128)(2,1)} %param.13), kind=kOutput, calls=%fused_computation.5 | convolution fusion | flops 6051102720 | bytes 40759296 | tf_op jit(solution)/shard_map/dot_general | solution.py:44
  65.7 0.4 fusion.35
  66.1 0.2 select_reduce_fusion
  66.3 0.2 fusion.15
  66.5 57.8 %all-reduce = f32[32,32]{1,0:T(8,128)S(1)} all-reduce(f32[32,32]{1,0:T(8,128)S(1)} %fusion.15), channel_id=2, replica_groups=mesh['pass'=16,'voc'=2] {'pass'}, use_global_device_ids=true, to_apply=%region_4.5.clone | all-reduce | flops 1024 | bytes 8192
  124.4 0.6 dynamic-slice
  125.6 4.9 %psum.14 = f32[2,32]{1,0:T(2,128)S(1)} all-reduce(f32[2,32]{1,0:T(2,128)S(1)} %constant_dynamic-slice_fusion), channel_id=1, replica_groups=mesh['pass'=16,'voc'=2] {'voc'}, use_global_device_ids=true, to_apply=%region_5.6 | all-reduce | flops 64 | bytes 512 | tf_op jit(solution)/shard_map/psum | solution.py:10
  130.5 0.1 reduce_max.9
  130.7 0.2 fusion.28
  130.9 0.1 constant_dynamic-update-slice_fusion.15
  131.0 0.0 collective-permute-start
  131.3 5.4 %collective-permute-done = f32[2,32]{1,0:T(2,128)S(1)} collective-permute-done((f32[2,32]{1,0:T(2,128)S(1)}, f32[2,32]{1,0:T(2,128)S(1)}, u32[]{:S(2)}, u32[]{:S(2)}) %collective-permute-start) | collective-permute-done | bytes 288 | tf_op jit(solution)/shard_map/ppermute | solution.py:61
  136.7 5.7 %collective-permute-done.1 = f32[2,32]{1,0:T(2,128)S(1)} collective-permute-done((f32[2,32]{1,0:T(2,128)S(1)}, f32[2,32]{1,0:T(2,128)S(1)}, u32[]{:S(2)}, u32[]{:S(2)}) %collective-permute-start.1) | collective-permute-done | bytes 288 | tf_op jit(solution)/shard_map/ppermute | solution.py:61
  142.4 5.7 %collective-permute-done.2 = f32[2,32]{1,0:T(2,128)S(1)} collective-permute-done((f32[2,32]{1,0:T(2,128)S(1)}, f32[2,32]{1,0:T(2,128)S(1)}, u32[]{:S(2)}, u32[]{:S(2)}) %collective-permute-start.2) | collective-permute-done | bytes 288 | tf_op jit(solution)/shard_map/ppermute | solution.py:61
  148.1 5.7 %collective-permute-done.3 = f32[2,32]{1,0:T(2,128)S(1)} collective-permute-done((f32[2,32]{1,0:T(2,128)S(1)}, f32[2,32]{1,0:T(2,128)S(1)}, u32[]{:S(2)}, u32[]{:S(2)}) %collective-permute-start.3) | collective-permute-done | bytes 288 | tf_op jit(solution)/shard_map/ppermute | solution.py:61
  153.8 5.7 %collective-permute-done.4 = f32[2,32]{1,0:T(2,128)S(1)} collective-permute-done((f32[2,32]{1,0:T(2,128)S(1)}, f32[2,32]{1,0:T(2,128)S(1)}, u32[]{:S(2)}, u32[]{:S(2)}) %collective-permute-start.4) | collective-permute-done | bytes 288 | tf_op jit(solution)/shard_map/ppermute | solution.py:61
  159.5 5.7 %collective-permute-done.5 = f32[2,32]{1,0:T(2,128)S(1)} collective-permute-done((f32[2,32]{1,0:T(2,128)S(1)}, f32[2,32]{1,0:T(2,128)S(1)}, u32[]{:S(2)}, u32[]{:S(2)}) %collective-permute-start.5) | collective-permute-done | bytes 288 | tf_op jit(solution)/shard_map/ppermute | solution.py:61
  165.1 5.7 %collective-permute-done.6 = f32[2,32]{1,0:T(2,128)S(1)} collective-permute-done((f32[2,32]{1,0:T(2,128)S(1)}, f32[2,32]{1,0:T(2,128)S(1)}, u32[]{:S(2)}, u32[]{:S(2)}) %collective-permute-start.6) | collective-permute-done | bytes 288 | tf_op jit(solution)/shard_map/ppermute | solution.py:61
  170.8 5.7 %collective-permute-done.7 = f32[2,32]{1,0:T(2,128)S(1)} collective-permute-done((f32[2,32]{1,0:T(2,128)S(1)}, f32[2,32]{1,0:T(2,128)S(1)}, u32[]{:S(2)}, u32[]{:S(2)}) %collective-permute-start.7) | collective-permute-done | bytes 288 | tf_op jit(solution)/shard_map/ppermute | solution.py:61
  176.5 5.7 %collective-permute-done.8 = f32[2,32]{1,0:T(2,128)S(1)} collective-permute-done((f32[2,32]{1,0:T(2,128)S(1)}, f32[2,32]{1,0:T(2,128)S(1)}, u32[]{:S(2)}, u32[]{:S(2)}) %collective-permute-start.8) | collective-permute-done | bytes 288 | tf_op jit(solution)/shard_map/ppermute | solution.py:61
  182.2 5.7 %collective-permute-done.9 = f32[2,32]{1,0:T(2,128)S(1)} collective-permute-done((f32[2,32]{1,0:T(2,128)S(1)}, f32[2,32]{1,0:T(2,128)S(1)}, u32[]{:S(2)}, u32[]{:S(2)}) %collective-permute-start.9) | collective-permute-done | bytes 288 | tf_op jit(solution)/shard_map/ppermute | solution.py:61
  187.9 5.7 %collective-permute-done.10 = f32[2,32]{1,0:T(2,128)S(1)} collective-permute-done((f32[2,32]{1,0:T(2,128)S(1)}, f32[2,32]{1,0:T(2,128)S(1)}, u32[]{:S(2)}, u32[]{:S(2)}) %collective-permute-start.10) | collective-permute-done | bytes 288 | tf_op jit(solution)/shard_map/ppermute | solution.py:61
  193.6 5.7 %collective-permute-done.11 = f32[2,32]{1,0:T(2,128)S(1)} collective-permute-done((f32[2,32]{1,0:T(2,128)S(1)}, f32[2,32]{1,0:T(2,128)S(1)}, u32[]{:S(2)}, u32[]{:S(2)}) %collective-permute-start.11) | collective-permute-done | bytes 288 | tf_op jit(solution)/shard_map/ppermute | solution.py:61
  199.3 5.7 %collective-permute-done.12 = f32[2,32]{1,0:T(2,128)S(1)} collective-permute-done((f32[2,32]{1,0:T(2,128)S(1)}, f32[2,32]{1,0:T(2,128)S(1)}, u32[]{:S(2)}, u32[]{:S(2)}) %collective-permute-start.12) | collective-permute-done | bytes 288 | tf_op jit(solution)/shard_map/ppermute | solution.py:61
  205.0 5.7 %collective-permute-done.13 = f32[2,32]{1,0:T(2,128)S(1)} collective-permute-done((f32[2,32]{1,0:T(2,128)S(1)}, f32[2,32]{1,0:T(2,128)S(1)}, u32[]{:S(2)}, u32[]{:S(2)}) %collective-permute-start.13) | collective-permute-done | bytes 288 | tf_op jit(solution)/shard_map/ppermute | solution.py:61
  210.7 5.7 %collective-permute-done.14 = f32[2,32]{1,0:T(2,128)S(1)} collective-permute-done((f32[2,32]{1,0:T(2,128)S(1)}, f32[2,32]{1,0:T(2,128)S(1)}, u32[]{:S(2)}, u32[]{:S(2)}) %collective-permute-start.14) | collective-permute-done | bytes 288 | tf_op jit(solution)/shard_map/ppermute | solution.py:61
  216.4 0.2 fusion.13
  216.6 0.9 fusion.34
  217.5 0.0 copy-start.1
  217.6 16.1 %fusion.7 = bf16[32,8,768]{2,1,0:T(8,128)(2,1)} fusion(bf16[768,15360]{1,0:T(8,128)(2,1)} %param.13, f32[256,15360]{1,0:T(8,128)} %get-tuple-element.5, f32[32,15360]{1,0:T(8,128)S(1)} %fusion.34), kind=kOutput, calls=%fused_computation.9 | convolution fusion | flops 6063587328 | bytes 41680896 | tf_op jit(solution)/shard_map/dot_general | solution.py:72
  233.7 0.0 all-reduce.3.cloned.1.call-update
  233.7 0.1 copy.20
  233.8 23.1 %all-reduce.3.cloned.1.call-done = bf16[32,8,768]{2,1,0:T(8,128)(2,1)} async-done(((bf16[32,8,768]{2,1,0:T(8,128)(2,1)}), bf16[32,8,768]{2,1,0:T(8,128)(2,1)}) %all-reduce.3.cloned.1.call-update) | async-done | bytes 393232 | tf_op jit(solution)/shard_map/psum | solution.py:78
  256.9 2.6 convolution_convert_fusion
  (41 shorter events, 0.2 us)
Async XLA Ops:
  7.2 28.6 %copy-start = (bf16[32,16,768]{2,1,0:T(8,128)(2,1)S(1)}, bf16[32,16,768]{2,1,0:T(8,128)(2,1)}, u32[]{:S(2)}) copy-start(bf16[32,16,768]{2,1,0:T(8,128)(2,1)} %param.8) | copy-start | bytes 2359300
  7.2 249.7 %all-reduce.3.cloned.1.call-start = ((), (), s32[]{:S(2)}) async-start(), calls=%async_computation | async-start | bytes 786432 | tf_op jit(solution)/shard_map/psum | solution.py:78
  38.2 27.9 %copy-start.4 = (s32[512]{0:T(512)S(1)}, s32[512]{0:T(512)}, u32[]{:S(2)}) copy-start(s32[512]{0:T(512)} %param.12) | copy-start | bytes 6148
  38.3 28.1 %copy-start.3 = (f32[32]{0:T(128)S(1)}, f32[32]{0:T(128)}, u32[]{:S(2)}) copy-start(f32[32]{0:T(128)} %param.10) | copy-start | bytes 388
  38.3 86.1 %copy-start.5 = (u32[32]{0:T(128)S(1)}, u32[32]{0:T(128)}, u32[]{:S(2)}) copy-start(u32[32]{0:T(128)} %constant.158) | copy-start | bytes 388
  130.5 103.1 %copy-start.2 = (f32[2,32]{1,0:T(2,128)}, f32[2,32]{1,0:T(2,128)S(1)}, u32[]{:S(2)}) copy-start(f32[2,32]{1,0:T(2,128)S(1)} %psum.14) | copy-start | bytes 772
  131.0 5.7 %collective-permute-start = (f32[2,32]{1,0:T(2,128)S(1)}, f32[2,32]{1,0:T(2,128)S(1)}, u32[]{:S(2)}, u32[]{:S(2)}) collective-permute-start(f32[2,32]{1,0:T(2,128)S(1)} %get-tuple-element.3), channel_id=1, source_target_pairs={{0,2},{2,4},{4,6},{6,8},{8,10},{10,12},{12,14},{14,16},{16,18},{18... | collective-permute-start | bytes 776 | tf_op jit(solution)/shard_map/ppermute | solution.py:61
  136.7 5.7 %collective-permute-start.1 = (f32[2,32]{1,0:T(2,128)S(1)}, f32[2,32]{1,0:T(2,128)S(1)}, u32[]{:S(2)}, u32[]{:S(2)}) collective-permute-start(f32[2,32]{1,0:T(2,128)S(1)} %collective-permute-done), channel_id=1, source_target_pairs={{0,2},{2,4},{4,6},{6,8},{8,10},{10,12},{12,14},{14,16},{16,18},{18... | collective-permute-start | bytes 776 | tf_op jit(solution)/shard_map/ppermute | solution.py:61
  142.3 5.7 %collective-permute-start.2 = (f32[2,32]{1,0:T(2,128)S(1)}, f32[2,32]{1,0:T(2,128)S(1)}, u32[]{:S(2)}, u32[]{:S(2)}) collective-permute-start(f32[2,32]{1,0:T(2,128)S(1)} %collective-permute-done.1), channel_id=1, source_target_pairs={{0,2},{2,4},{4,6},{6,8},{8,10},{10,12},{12,14},{14,16},{16,18},{18... | collective-permute-start | bytes 776 | tf_op jit(solution)/shard_map/ppermute | solution.py:61
  148.0 5.7 %collective-permute-start.3 = (f32[2,32]{1,0:T(2,128)S(1)}, f32[2,32]{1,0:T(2,128)S(1)}, u32[]{:S(2)}, u32[]{:S(2)}) collective-permute-start(f32[2,32]{1,0:T(2,128)S(1)} %collective-permute-done.2), channel_id=1, source_target_pairs={{0,2},{2,4},{4,6},{6,8},{8,10},{10,12},{12,14},{14,16},{16,18},{18... | collective-permute-start | bytes 776 | tf_op jit(solution)/shard_map/ppermute | solution.py:61
  153.7 5.7 %collective-permute-start.4 = (f32[2,32]{1,0:T(2,128)S(1)}, f32[2,32]{1,0:T(2,128)S(1)}, u32[]{:S(2)}, u32[]{:S(2)}) collective-permute-start(f32[2,32]{1,0:T(2,128)S(1)} %collective-permute-done.3), channel_id=1, source_target_pairs={{0,2},{2,4},{4,6},{6,8},{8,10},{10,12},{12,14},{14,16},{16,18},{18... | collective-permute-start | bytes 776 | tf_op jit(solution)/shard_map/ppermute | solution.py:61
  159.4 5.7 %collective-permute-start.5 = (f32[2,32]{1,0:T(2,128)S(1)}, f32[2,32]{1,0:T(2,128)S(1)}, u32[]{:S(2)}, u32[]{:S(2)}) collective-permute-start(f32[2,32]{1,0:T(2,128)S(1)} %collective-permute-done.4), channel_id=1, source_target_pairs={{0,2},{2,4},{4,6},{6,8},{8,10},{10,12},{12,14},{14,16},{16,18},{18... | collective-permute-start | bytes 776 | tf_op jit(solution)/shard_map/ppermute | solution.py:61
  165.1 5.7 %collective-permute-start.6 = (f32[2,32]{1,0:T(2,128)S(1)}, f32[2,32]{1,0:T(2,128)S(1)}, u32[]{:S(2)}, u32[]{:S(2)}) collective-permute-start(f32[2,32]{1,0:T(2,128)S(1)} %collective-permute-done.5), channel_id=1, source_target_pairs={{0,2},{2,4},{4,6},{6,8},{8,10},{10,12},{12,14},{14,16},{16,18},{18... | collective-permute-start | bytes 776 | tf_op jit(solution)/shard_map/ppermute | solution.py:61
  170.8 5.7 %collective-permute-start.7 = (f32[2,32]{1,0:T(2,128)S(1)}, f32[2,32]{1,0:T(2,128)S(1)}, u32[]{:S(2)}, u32[]{:S(2)}) collective-permute-start(f32[2,32]{1,0:T(2,128)S(1)} %collective-permute-done.6), channel_id=1, source_target_pairs={{0,2},{2,4},{4,6},{6,8},{8,10},{10,12},{12,14},{14,16},{16,18},{18... | collective-permute-start | bytes 776 | tf_op jit(solution)/shard_map/ppermute | solution.py:61
  176.5 5.7 %collective-permute-start.8 = (f32[2,32]{1,0:T(2,128)S(1)}, f32[2,32]{1,0:T(2,128)S(1)}, u32[]{:S(2)}, u32[]{:S(2)}) collective-permute-start(f32[2,32]{1,0:T(2,128)S(1)} %collective-permute-done.7), channel_id=1, source_target_pairs={{0,2},{2,4},{4,6},{6,8},{8,10},{10,12},{12,14},{14,16},{16,18},{18... | collective-permute-start | bytes 776 | tf_op jit(solution)/shard_map/ppermute | solution.py:61
  182.2 5.7 %collective-permute-start.9 = (f32[2,32]{1,0:T(2,128)S(1)}, f32[2,32]{1,0:T(2,128)S(1)}, u32[]{:S(2)}, u32[]{:S(2)}) collective-permute-start(f32[2,32]{1,0:T(2,128)S(1)} %collective-permute-done.8), channel_id=1, source_target_pairs={{0,2},{2,4},{4,6},{6,8},{8,10},{10,12},{12,14},{14,16},{16,18},{18... | collective-permute-start | bytes 776 | tf_op jit(solution)/shard_map/ppermute | solution.py:61
  187.9 5.7 %collective-permute-start.10 = (f32[2,32]{1,0:T(2,128)S(1)}, f32[2,32]{1,0:T(2,128)S(1)}, u32[]{:S(2)}, u32[]{:S(2)}) collective-permute-start(f32[2,32]{1,0:T(2,128)S(1)} %collective-permute-done.9), channel_id=1, source_target_pairs={{0,2},{2,4},{4,6},{6,8},{8,10},{10,12},{12,14},{14,16},{16,18},{18... | collective-permute-start | bytes 776 | tf_op jit(solution)/shard_map/ppermute | solution.py:61
  193.6 5.7 %collective-permute-start.11 = (f32[2,32]{1,0:T(2,128)S(1)}, f32[2,32]{1,0:T(2,128)S(1)}, u32[]{:S(2)}, u32[]{:S(2)}) collective-permute-start(f32[2,32]{1,0:T(2,128)S(1)} %collective-permute-done.10), channel_id=1, source_target_pairs={{0,2},{2,4},{4,6},{6,8},{8,10},{10,12},{12,14},{14,16},{16,18},{18... | collective-permute-start | bytes 776 | tf_op jit(solution)/shard_map/ppermute | solution.py:61
  199.3 5.7 %collective-permute-start.12 = (f32[2,32]{1,0:T(2,128)S(1)}, f32[2,32]{1,0:T(2,128)S(1)}, u32[]{:S(2)}, u32[]{:S(2)}) collective-permute-start(f32[2,32]{1,0:T(2,128)S(1)} %collective-permute-done.11), channel_id=1, source_target_pairs={{0,2},{2,4},{4,6},{6,8},{8,10},{10,12},{12,14},{14,16},{16,18},{18... | collective-permute-start | bytes 776 | tf_op jit(solution)/shard_map/ppermute | solution.py:61
  205.0 5.7 %collective-permute-start.13 = (f32[2,32]{1,0:T(2,128)S(1)}, f32[2,32]{1,0:T(2,128)S(1)}, u32[]{:S(2)}, u32[]{:S(2)}) collective-permute-start(f32[2,32]{1,0:T(2,128)S(1)} %collective-permute-done.12), channel_id=1, source_target_pairs={{0,2},{2,4},{4,6},{6,8},{8,10},{10,12},{12,14},{14,16},{16,18},{18... | collective-permute-start | bytes 776 | tf_op jit(solution)/shard_map/ppermute | solution.py:61
  210.7 5.7 %collective-permute-start.14 = (f32[2,32]{1,0:T(2,128)S(1)}, f32[2,32]{1,0:T(2,128)S(1)}, u32[]{:S(2)}, u32[]{:S(2)}) collective-permute-start(f32[2,32]{1,0:T(2,128)S(1)} %collective-permute-done.13), channel_id=1, source_target_pairs={{0,2},{2,4},{4,6},{6,8},{8,10},{10,12},{12,14},{14,16},{16,18},{18... | collective-permute-start | bytes 776 | tf_op jit(solution)/shard_map/ppermute | solution.py:61
  217.5 16.2 %copy-start.1 = (s32[32,8]{0,1:T(8,128)S(1)}, s32[32,8]{0,1:T(8,128)}, u32[]{:S(2)}) copy-start(s32[32,8]{0,1:T(8,128)} %param.9) | copy-start | bytes 3076
Sparse Core Ops, SparseCore 0:
  233.8 23.0 all-reduce.2
